TPU v7x, 256 devices: a whole 4x4x8 slice. The times are simulated.
256 devices in a mesh: depth: 8 (over z), lateral: 32 (over x, y, core).
Axes of the slice: x: 4, y: 4, z: 8, core: 2. Of those that a mesh axis runs over, the one named last changes fastest.
Arguments:
- samples: bfloat16 [8, 32, 64, 8192], P('depth', 'lateral'), may hold values from -6 to 6
- w_first: bfloat16 [8, 32, 64, 256], P('depth', 'lateral'), may hold values from -0.75 to 0.75
- w_second: bfloat16 [8, 32, 256, 256], P('depth', 'lateral'), may hold values from -0.5 to 0.5
- w_third: bfloat16 [8, 32, 256, 512], P('depth', 'lateral'), may hold values from -0.5 to 0.5
- w_density: bfloat16 [8, 32, 256], P('depth', 'lateral'), may hold values from -0.5 to 0.5
- decoder: float32 [32, 3, 512], P('lateral'), may hold values from -1 to 1
- depth_order: int32 [32, 8], P('lateral'), may hold values from 0 to 7, each once within a row
- ray_slot: int32 [32, 1024], P('lateral'), may hold values from 0 to 127, as said below
- target: float32 [32, 3, 256], P('lateral', None, 'depth'), may hold values from -24 to 24
Outputs:
- grad_first: float32 [8, 32, 64, 256], P('depth', 'lateral')
- grad_second: float32 [8, 32, 256, 256], P('depth', 'lateral')
- grad_third: float32 [8, 32, 256, 512], P('depth', 'lateral')
- grad_density: float32 [8, 32, 256], P('depth', 'lateral')
- grad_decoder: float32 [32, 3, 512], P('lateral')
- mean_error: float32 [], replicated
Inputs may be any that keep to these rules, and one draw needn't show every extreme that they name: `ray_slot`: in each row, every aligned block of 128 entries holds each of 0 to 127 once. `depth_order`: each row names every tile once.
All inputs are finite; a program needn't handle non-finite values.
Results may differ from a plain program's by a relative error of at most 0.017.
The roundings to bfloat16 on the way count: a program that leaves them out, or rounds other values in their place, can miss the bound.
Values may be sent and summed in bfloat16 or wider, within the bound.
A program may use at most 128 MiB of HBM per device.

v0:
```python
import jax
import jax.numpy as jnp
from jax import lax
from jax.experimental import pallas as pl
from jax.experimental.pallas import tpu as pltpu
from jax.sharding import PartitionSpec as P

MESH = pl.DeviceIdType.MESH
F32 = jnp.float32
BF16 = jnp.bfloat16

ENC, HID, FEAT = 64, 256, 512
S = 8
K = 8
R = 128
CHIPS = 16
W = S * R
HALF = FEAT // 2
STEP = 0.04
FLOOR = 1e-05
COUNT = 24576.0
LAG = 3

NN = (((1,), (0,)), ((), ()))
NT = (((1,), (1,)), ((), ()))
TN = (((0,), (0,)), ((), ()))


def mm(a, b, dims):
    return lax.dot_general(a, b, dims, preferred_element_type=F32)


def offset_of(i):
    return 4 + ((i + 1) // 2) * (1 - 2 * (i % 2))


def near_offset_of(i):
    return ((i + 1) // 2) * (2 * (i % 2) - 1) + 8


def kernel(
    x_ref, w1_ref, w2_ref, w3_ref, wd_ref, dec_ref, order_ref, slot_ref, tgt_ref,
    g1_ref, g2_ref, g3_ref, gd_ref, gdec_ref, err_ref,
    w1t, w2t, w3t, wdb, h1s, h2s, feats, lgs, wts, expi, bld, scl, scaled, oh,
    pfull, prec, zsend, zrecv, lt, lr, lb, br, gbuf, dsall, tmall, wgs, lgrad, b2s,
    decall, esend, elat, epsend, eprec,
    s_ds, r_ds, s_pf, r_pf, s_z, r_z, s_l, r_l, s_b, r_b, s_g, r_g, s_pb, r_pb,
    s_t, r_t, s_d, r_d, s_e, r_e, s_ep, r_ep,
):
    me = lax.axis_index("depth")
    lat = lax.axis_index("lateral")
    h = lat % 2
    m = lat // 2
    sib = lat + 1 - 2 * h

    def depth_peer(off):
        return (me + off) % K

    def rc(src, dst, ssem, rsem, z, l):
        return pltpu.make_async_remote_copy(
            src_ref=src, dst_ref=dst, send_sem=ssem, recv_sem=rsem,
            device_id=(z, l), device_id_type=MESH,
        )

    barrier = pltpu.get_barrier_semaphore()

    def greet_depth(e, c):
        pl.semaphore_signal(barrier, inc=1, device_id=((me + e) % K, lat), device_id_type=MESH)
        return c

    def greet_lateral(e, c):
        pl.semaphore_signal(
            barrier, inc=1, device_id=(me, ((m + e) % CHIPS) * 2 + h), device_id_type=MESH
        )
        return c

    lax.fori_loop(1, K, greet_depth, 0)
    lax.fori_loop(1, CHIPS, greet_lateral, 0)
    pl.semaphore_signal(barrier, inc=1, device_id=(me, sib), device_id_type=MESH)

    w1t[...] = w1_ref[...].T
    w2t[...] = w2_ref[...].T
    w3t[...] = w3_ref[...].T
    wd8 = jnp.broadcast_to(wd_ref[...], (8, HID))
    wdb[...] = jnp.broadcast_to(wd_ref[...].astype(F32), (R, HID)).T

    def take_x(d):
        return jnp.concatenate(
            [x_ref[:, pl.ds(pl.multiple_of(s * (K * R) + d * R, R), R)] for s in range(S)], axis=1
        )

    def first_pass(d, c):
        x = take_x(d)
        h1s[d] = jnp.maximum(mm(w1t[...], x, NN), 0.0).astype(BF16)
        h2s[d] = jnp.maximum(mm(w2t[...], h1s[d], NN), 0.0).astype(BF16)
        lg = mm(wd8, h2s[d], NN)
        lgs[d] = jnp.concatenate(
            [lg[s : s + 1, s * R : (s + 1) * R] for s in range(S)], axis=0
        )
        return c

    lax.fori_loop(0, K, first_pass, 0)

    sub = lax.broadcasted_iota(jnp.int32, (K, S, R), 1)
    logits = lgs[...]
    density = jnp.maximum(logits, 0.0) + jnp.log1p(jnp.exp(-jnp.abs(logits)))
    inc = density
    for sh in (1, 2, 4):
        inc = inc + jnp.where(sub >= sh, pltpu.roll(inc, sh, 1), 0.0)
    wts[...] = jnp.exp(-STEP * (inc - density)) * (1.0 - jnp.exp(-STEP * density))
    expi[...] = jnp.exp(-STEP * inc)
    dsall[me] = STEP * jnp.concatenate([inc[d, S - 1 : S, :] for d in range(K)], axis=0)

    pl.semaphore_wait(barrier, K - 1 + CHIPS - 1 + 1)

    def ds_copy(off, k):
        return rc(dsall.at[k], dsall.at[k], s_ds.at[off], r_ds.at[k], depth_peer(off), lat)

    def send_ds(off, c):
        ds_copy(off, me).start()
        return c

    lax.fori_loop(1, K, send_ds, 0)

    row = lax.broadcasted_iota(jnp.int32, (2 * R, R), 0)
    code = (((row // 8) % CHIPS) * 2 + row // R) * 4 + row % 4
    code_lo = jnp.where((row // 4) % 2 == 0, code, -1)
    code_hi = jnp.where((row // 4) % 2 == 1, code, -1)

    def one_hot(d, c):
        slots = slot_ref[:, pl.ds(pl.multiple_of(d * R, R), R)]
        oh[d] = jnp.concatenate(
            [
                jnp.where(code_lo == slots, 1.0, 0.0).astype(BF16),
                jnp.where(code_hi == slots, 1.0, 0.0).astype(BF16),
            ],
            axis=1,
        )
        return c

    lax.fori_loop(0, K, one_hot, 0)

    def second_pass(d, c):
        feats[d] = mm(w3t[...], h2s[d], NN).astype(BF16)
        for f0 in range(0, FEAT, 64):
            total = jnp.zeros((64, R), F32)
            for s in range(S):
                total = total + feats[d, f0 : f0 + 64, s * R : (s + 1) * R].astype(F32) * wts[
                    d, s : s + 1, :
                ]
            fh = f0 // HALF
            bld[d, f0 - fh * HALF : f0 - fh * HALF + 64, fh * R : (fh + 1) * R] = total
        return c

    lax.fori_loop(0, K, second_pass, 0)

    places = []
    mine = jnp.int32(0)
    for k in range(K):
        place = jnp.int32(0)
        for p in range(K):
            place = place + jnp.where(order_ref[0, p] == k, p, 0)
        places.append(place)
    for p in range(K):
        mine = mine + jnp.where(order_ref[0, p] == me, p, 0)

    def wait_ds(off, c):
        ds_copy(off, depth_peer(off)).wait_recv()
        return c

    lax.fori_loop(1, K, wait_ds, 0)
    before = jnp.zeros((K, R), F32)
    for k in range(K):
        before = before + dsall[k] * jnp.where(places[k] < mine, 1.0, 0.0)
    scl[...] = jnp.exp(-before)

    def pf_copy(d):
        return rc(pfull.at[d, 1 - h], prec.at[d], s_pf.at[d], r_pf.at[d], me, sib)

    def z_copy(d, k):
        return rc(zsend.at[d], zrecv.at[k], s_z.at[d], r_z.at[k], d, lat)

    def make_scaled(d):
        sc = scl[pl.ds(d, 1), :]
        sc = jnp.concatenate([sc, sc], axis=1)
        scaled[d] = (bld[d] * sc).astype(BF16)
        placed = mm(oh[d], scaled[d], NT).astype(BF16)
        pfull[d, 0] = placed[0:R]
        pfull[d, 1] = placed[R : 2 * R]
        pf_copy(d).start()

    def pair_sum(d):
        pf_copy(d).wait_recv()
        return (pfull[d, h].astype(F32) + prec[d].astype(F32)).astype(BF16)

    def send_share(i):
        d = depth_peer(offset_of(i))
        zsend[d] = pair_sum(d)
        z_copy(d, me).start()

    def scaled_step(i, c):
        make_scaled(depth_peer(offset_of(i)))

        @pl.when(i >= LAG)
        def _():
            send_share(i - LAG)

        return c

    lax.fori_loop(0, K, scaled_step, 0)
    for i in range(K - LAG, K - 1):
        send_share(i)
    zrecv[me] = pair_sum(me)

    def wait_z(off, c):
        z_copy(me, depth_peer(off)).wait_recv()
        return c

    lax.fori_loop(1, K, wait_z, 0)
    total = zrecv[0].astype(F32)
    for k in range(1, K):
        total = total + zrecv[k].astype(F32)
    lt[...] = total.reshape(CHIPS, 8, HALF)

    def l_copy(e, src):
        to = (m + e) % CHIPS
        return rc(lt.at[to], lr.at[src], s_l.at[to], r_l.at[src], me, to * 2 + h)

    def send_l(e, c):
        l_copy(e, m).start()
        return c

    lax.fori_loop(1, CHIPS, send_l, 0)
    lr[m] = lt[m]

    shape3 = (8, 8, 32)
    grp = lax.broadcasted_iota(jnp.int32, shape3, 0)
    rowq = lax.broadcasted_iota(jnp.int32, shape3, 1) % 4
    pix = lax.broadcasted_iota(jnp.int32, shape3, 2)
    chosen = pix == rowq * 8 + grp
    low = lax.broadcasted_iota(jnp.int32, (8, HALF), 0) < 4
    targets = []
    decs = []
    for i in range(3):
        t = jnp.where(chosen, jnp.broadcast_to(tgt_ref[i : i + 1, :][None], shape3), 0.0)
        targets.append(jnp.sum(t, axis=2, keepdims=True))
        decs.append(
            jnp.where(
                low,
                jnp.broadcast_to(dec_ref[i : i + 1, 0:HALF], (8, HALF)),
                jnp.broadcast_to(dec_ref[i : i + 1, HALF:FEAT], (8, HALF)),
            )[None]
        )

    def both_halves(v):
        v = jnp.broadcast_to(jnp.sum(v, axis=2, keepdims=True), (8, 8, R))
        return v + pltpu.roll(v, 4, 1)

    def wide(v):
        return jnp.concatenate([v, v], axis=2)

    def wait_l(e, c):
        l_copy(e, (m + e) % CHIPS).wait_recv()
        return c

    lax.fori_loop(1, CHIPS, wait_l, 0)
    arrived = lr[...].reshape(8, 2, 8, HALF)
    mean = (arrived[:, 0] + arrived[:, 1]) * 0.25
    inverse = wide(lax.rsqrt(both_halves(mean * mean) * (1.0 / FEAT) + FLOOR))
    normed = mean * inverse
    normed_grad = jnp.zeros((8, 8, HALF), F32)
    square = jnp.zeros((8, 8, R), F32)
    dec_rows = []
    for i in range(3):
        residue = both_halves(normed * decs[i]) - targets[i]
        square = square + residue * residue
        res_wide = wide(residue)
        normed_grad = normed_grad + decs[i] * res_wide
        part = jnp.sum(res_wide * normed, axis=0)
        dec_rows.append(jnp.sum(part[0:4], axis=0, keepdims=True))
        dec_rows.append(jnp.sum(part[4:8], axis=0, keepdims=True))
    along = wide(both_halves(normed_grad * normed)) * (1.0 / FEAT)
    pixel_grad = inverse * (normed_grad - normed * along) * 0.25
    lb[...] = pixel_grad.astype(BF16).astype(F32)

    def b_copy(e, src):
        to = (m + e) % CHIPS
        return rc(lb.at[to // 2], br.at[src], s_b.at[to], r_b.at[src], me, to * 2 + h)

    def send_b(e, c):
        b_copy(e, m).start()
        return c

    lax.fori_loop(1, CHIPS, send_b, 0)
    br[m] = lb[m // 2]

    err_row = jnp.sum(jnp.sum(square, axis=0), axis=0, keepdims=True) * 0.5
    dec_rows.append(jnp.concatenate([err_row, err_row], axis=1))
    dec_rows.append(jnp.zeros((1, HALF), F32))
    decall[me] = jnp.concatenate(dec_rows, axis=0)

    def wait_b(e, c):
        b_copy(e, (m + e) % CHIPS).wait_recv()
        return c

    lax.fori_loop(1, CHIPS, wait_b, 0)
    gbuf[me, h] = br[...].reshape(R, HALF).astype(BF16)

    def g_copy(off, k):
        return rc(gbuf.at[k, h], gbuf.at[k, h], s_g.at[off], r_g.at[k], depth_peer(off), lat)

    def pb_copy(d, half):
        return rc(gbuf.at[d, half], gbuf.at[d, half], s_pb.at[d], r_pb.at[d], me, sib)

    def d_copy(off, k):
        return rc(decall.at[k], decall.at[k], s_d.at[off], r_d.at[k], depth_peer(off), lat)

    def send_g(i, c):
        g_copy(offset_of(i), me).start()
        return c

    lax.fori_loop(0, K - 1, send_g, 0)

    def send_d(off, c):
        d_copy(off, me).start()
        return c

    lax.fori_loop(1, K, send_d, 0)

    def take_share(i):
        d = depth_peer(near_offset_of(i))

        @pl.when(i > 0)
        def _():
            g_copy(near_offset_of(i) % K, d).wait_recv()

        pb_copy(d, h).start()

    def back_share(i):
        d = depth_peer(near_offset_of(i))
        pb_copy(d, 1 - h).wait_recv()
        grads = gbuf[d].reshape(2 * R, HALF)
        ray_grad = mm(grads, oh[d], TN)
        terms = jnp.sum(scaled[d].astype(F32) * ray_grad, axis=0, keepdims=True)
        tmall[me, pl.ds(d, 1), :] = terms[:, 0:R] + terms[:, R : 2 * R]
        sc = scl[pl.ds(d, 1), :]
        bld[d] = ray_grad * jnp.concatenate([sc, sc], axis=1)
        weight_grad = [jnp.zeros((8, R), F32) for _ in range(S)]
        for f0 in range(0, FEAT, 64):
            fh = f0 // HALF
            fg = bld[d, f0 - fh * HALF : f0 - fh * HALF + 64, fh * R : (fh + 1) * R]
            for s in range(S):
                part = feats[d, f0 : f0 + 64, s * R : (s + 1) * R].astype(F32) * fg
                weight_grad[s] = weight_grad[s] + jnp.sum(part.reshape(8, 8, R), axis=0)
                feats[d, f0 : f0 + 64, s * R : (s + 1) * R] = (
                    fg * wts[d, s : s + 1, :]
                ).astype(BF16)
        wgs[d] = jnp.concatenate(
            [jnp.sum(weight_grad[s], axis=0, keepdims=True) for s in range(S)], axis=0
        )

    def back_step(i, c):
        take_share(i)

        @pl.when(i >= 1)
        def _():
            back_share(i - 1)

        return c

    lax.fori_loop(0, K, back_step, 0)
    back_share(K - 1)

    def t_copy(off, k):
        return rc(tmall.at[k], tmall.at[k], s_t.at[off], r_t.at[k], depth_peer(off), lat)

    def send_t(off, c):
        t_copy(off, me).start()
        return c

    lax.fori_loop(1, K, send_t, 0)

    def wait_d(off, c):
        d_copy(off, depth_peer(off)).wait_recv()
        return c

    lax.fori_loop(1, K, wait_d, 0)
    dec_sum = decall[0]
    for k in range(1, K):
        dec_sum = dec_sum + decall[k]
    for i in range(3):
        gdec_ref[i : i + 1, 0:HALF] = dec_sum[2 * i : 2 * i + 1]
        gdec_ref[i : i + 1, HALF:FEAT] = dec_sum[2 * i + 1 : 2 * i + 2]
    esend[...] = jnp.broadcast_to(dec_sum[6:7, 0:R], (8, R))
    elat[m] = esend[...]

    def e_copy(e, src):
        to = (m + e) % CHIPS
        return rc(esend, elat.at[src], s_e.at[to], r_e.at[src], me, to * 2 + h)

    def send_e(e, c):
        e_copy(e, m).start()
        return c

    lax.fori_loop(1, CHIPS, send_e, 0)

    g3_ref[...] = jnp.zeros_like(g3_ref)

    def third_step(d, c):
        g3_ref[...] += mm(h2s[d], feats[d], NT)
        return c

    lax.fori_loop(0, K, third_step, 0)

    def wait_e(e, c):
        e_copy(e, (m + e) % CHIPS).wait_recv()
        return c

    lax.fori_loop(1, CHIPS, wait_e, 0)
    err_sum = elat[0]
    for k in range(1, CHIPS):
        err_sum = err_sum + elat[k]
    epsend[...] = err_sum
    ep_copy = rc(epsend, eprec, s_ep, r_ep, me, sib)
    ep_copy.start()

    def wait_t(off, c):
        t_copy(off, depth_peer(off)).wait_recv()
        return c

    lax.fori_loop(1, K, wait_t, 0)
    behind = jnp.zeros((K, R), F32)
    for k in range(K):
        behind = behind + tmall[k] * jnp.where(places[k] > mine, 1.0, 0.0)
    sub2 = lax.broadcasted_iota(jnp.int32, (S, R), 0)
    for d in range(K):
        wg = wgs[d]
        own = wg * wts[d]
        suffix = own
        for sh in (1, 2, 4):
            suffix = suffix + jnp.where(sub2 < S - sh, pltpu.roll(suffix, S - sh, 0), 0.0)
        density_grad = STEP * (wg * expi[d] - (suffix - own) - behind[d : d + 1, :])
        lg = lgs[d]
        sig = 1.0 / (1.0 + jnp.exp(-lg))
        lgrad[d] = (density_grad * sig).astype(BF16).astype(F32)

    g1_ref[...] = jnp.zeros_like(g1_ref)
    g2_ref[...] = jnp.zeros_like(g2_ref)

    def last_step(d, gdens):
        lg = lgrad[d]
        lg8 = jnp.concatenate(
            [jnp.broadcast_to(lg[s : s + 1, :], (8, R)) for s in range(S)], axis=1
        )
        gdens = gdens + mm(lg8.astype(BF16), h2s[d], NT)
        b2 = mm(w3_ref[...], feats[d], NN)
        for s in range(S):
            cols = slice(s * R, (s + 1) * R)
            v = b2[:, cols] + wdb[...] * lg[s : s + 1, :]
            b2s[:, cols] = jnp.where(h2s[d, :, cols].astype(F32) > 0.0, v, 0.0).astype(BF16)
        g2_ref[...] += mm(h1s[d], b2s[...], NT)
        b1 = mm(w2_ref[...], b2s[...], NN)
        b1 = jnp.where(h1s[d].astype(F32) > 0.0, b1, 0.0).astype(BF16)
        g1_ref[...] += mm(take_x(d), b1, NT)
        return gdens

    gdens = lax.fori_loop(0, K, last_step, jnp.zeros((8, HID), F32))
    gd_ref[...] = gdens[0:1]

    ep_copy.wait_recv()
    err_ref[...] = (epsend[0:1, 0:1] + eprec[0:1, 0:1]) * (1.0 / COUNT)

    def end_depth(off, c):
        d = depth_peer(off)
        ds_copy(off, me).wait_send()
        z_copy(d, me).wait_send()
        g_copy(off, me).wait_send()
        d_copy(off, me).wait_send()
        t_copy(off, me).wait_send()
        return c

    lax.fori_loop(1, K, end_depth, 0)

    def end_lateral(e, c):
        l_copy(e, m).wait_send()
        b_copy(e, m).wait_send()
        e_copy(e, m).wait_send()
        return c

    lax.fori_loop(1, CHIPS, end_lateral, 0)

    def end_pair(d, c):
        pf_copy(d).wait_send()
        pb_copy(d, h).wait_send()
        return c

    lax.fori_loop(0, K, end_pair, 0)
    ep_copy.wait_send()


def body(samples, w_first, w_second, w_third, w_density, decoder, depth_order, ray_slot, target):
    vmem = pl.BlockSpec(memory_space=pltpu.VMEM)
    dma = pltpu.SemaphoreType.DMA
    v = pltpu.VMEM
    outs = pl.pallas_call(
        kernel,
        name="step",
        out_shape=(
            jax.ShapeDtypeStruct((ENC, HID), F32),
            jax.ShapeDtypeStruct((HID, HID), F32),
            jax.ShapeDtypeStruct((HID, FEAT), F32),
            jax.ShapeDtypeStruct((1, HID), F32),
            jax.ShapeDtypeStruct((3, FEAT), F32),
            jax.ShapeDtypeStruct((1, 1), F32),
        ),
        in_specs=[vmem] * 6 + [pl.BlockSpec(memory_space=pltpu.SMEM)] + [vmem] * 2,
        out_specs=(vmem,) * 6,
        scratch_shapes=[
            v((HID, ENC), BF16),
            v((HID, HID), BF16),
            v((FEAT, HID), BF16),
            v((HID, R), F32),
            v((K, HID, W), BF16),
            v((K, HID, W), BF16),
            v((K, FEAT, W), BF16),
            v((K, S, R), F32),
            v((K, S, R), F32),
            v((K, S, R), F32),
            v((K, HALF, 2 * R), F32),
            v((K, R), F32),
            v((K, HALF, 2 * R), BF16),
            v((K, 2 * R, 2 * R), BF16),
            v((K, 2, R, HALF), BF16),
            v((K, R, HALF), BF16),
            v((K, R, HALF), BF16),
            v((K, R, HALF), BF16),
            v((CHIPS, 8, HALF), F32),
            v((CHIPS, 8, HALF), F32),
            v((8, 8, HALF), F32),
            v((CHIPS, 8, HALF), F32),
            v((K, 2, R, HALF), BF16),
            v((K, K, R), F32),
            v((K, K, R), F32),
            v((K, S, R), F32),
            v((K, S, R), F32),
            v((HID, W), BF16),
            v((K, 8, HALF), F32),
            v((8, R), F32),
            v((CHIPS, 8, R), F32),
            v((8, R), F32),
            v((8, R), F32),
            dma((K,)), dma((K,)),
            dma((K,)), dma((K,)),
            dma((K,)), dma((K,)),
            dma((CHIPS,)), dma((CHIPS,)),
            dma((CHIPS,)), dma((CHIPS,)),
            dma((K,)), dma((K,)),
            dma((K,)), dma((K,)),
            dma((K,)), dma((K,)),
            dma((K,)), dma((K,)),
            dma((CHIPS,)), dma((CHIPS,)),
            dma(()), dma(()),
        ],
        compiler_params=pltpu.CompilerParams(
            collective_id=0, has_side_effects=True, vmem_limit_bytes=58 * 1024 * 1024
        ),
    )(
        samples[0, 0],
        w_first[0, 0],
        w_second[0, 0],
        w_third[0, 0],
        w_density[0],
        decoder[0],
        depth_order,
        ray_slot,
        target[0],
    )
    return (
        outs[0][None, None],
        outs[1][None, None],
        outs[2][None, None],
        outs[3][None],
        outs[4][None],
        outs[5][0, 0],
    )


def solution(mesh):
    placed = (
        P("depth", "lateral", None, None),
        P("depth", "lateral", None, None),
        P("depth", "lateral", None, None),
        P("depth", "lateral", None, None),
        P("depth", "lateral", None),
        P("lateral", None, None),
        P("lateral", None),
        P("lateral", None),
        P("lateral", None, "depth"),
    )
    return jax.shard_map(
        body,
        mesh=mesh,
        in_specs=placed,
        out_specs=(
            P("depth", "lateral", None, None),
            P("depth", "lateral", None, None),
            P("depth", "lateral", None, None),
            P("depth", "lateral", None),
            P("lateral", None, None),
            P(),
        ),
        check_vma=False,
    )
```

profile of v0, /device:TPU:1, one launch (start us, length us, event | category | flops | bytes accessed | tf_op | source)
XLA Modules:
  0.0 90.4 jit_solution(13438545798916077199)
XLA Ops:
  0.6 0.0 copy-start.2
  0.6 0.0 copy-start.1
  0.7 0.7 copy-done.2
  1.3 0.6 copy.21
  1.9 0.0 copy-done.1
  1.9 0.6 copy.20
  2.5 80.2 %step.1 = (f32[64,256]{1,0:T(8,128)}, f32[256,256]{1,0:T(8,128)}, f32[256,512]{1,0:T(8,128)}, f32[1,256]{1,0:T(1,128)}, f32[3,512]{1,0:T(4,128)}, /*index=5*/f32[1,1]{1,0:T(1,128)}) custom-call(bf16[64,8192]{1,0:T(8,128)(2,1)} %bitcast.17, bf16[64,256]{1,0:T(8,128)(2,1)} %bitcast.24, bf16[256,256]{1,0:T(8,128)(2,1)} %bitcast.21, bf16[256,512]{1,0:T(8,128)(2,1)} %bitcast.20, ...), custom_call_target="tpu_custom_call" | custom-call | tf_op jit(solution)/shard_map/step/pallas_call | solution.py:505
  82.7 0.0 copy-start
  82.7 1.4 %copy.15 = f32[1,3,512]{2,0,1:T(1,128)} copy(f32[1,3,512]{2,1,0:T(4,128)} %bitcast.26) | data formatting | bytes 12288
  84.1 1.5 %copy.27 = f32[1,1,64,256]{3,2,1,0:T(8,128)} copy(f32[1,1,64,256]{3,2,1,0:T(8,128)} %bitcast.22) | data formatting | bytes 131072
  85.6 1.7 %copy.28 = f32[1,1,256,256]{3,2,1,0:T(8,128)} copy(f32[1,1,256,256]{3,2,1,0:T(8,128)} %bitcast.19) | data formatting | bytes 524288
  87.2 0.0 copy-done
  87.2 0.0 copy-start.3
  87.2 0.8 copy.29
  88.0 0.0 copy-done.3
  88.0 0.6 copy.30
Async XLA Ops:
  0.6 0.7 copy-start.2
  0.6 1.3 %copy-start.1 = (f32[1,3,512]{2,0,1:T(1,128)S(1)}, f32[1,3,512]{2,0,1:T(1,128)}, u32[]{:S(2)}) copy-start(f32[1,3,512]{2,0,1:T(1,128)} %param.14) | copy-start | bytes 18436
  82.7 4.5 %copy-start = (f32[256,512]{1,0:T(8,128)S(1)}, f32[256,512]{1,0:T(8,128)}, u32[]{:S(2)}) copy-start(f32[256,512]{1,0:T(8,128)} %get-tuple-element.14) | copy-start | bytes 1572868
  87.2 0.8 copy-start.3
where the time goes:
time: 90.6 us; the launch traced here: 90.4 us
  Pallas kernels  80.2 us (89%)
  local copies, waits for them, and re-layouts  7.7 us (8%)
  between operations  2.44 us (3%)
    pallas_call x1, Pallas kernels, body(): pl.pallas_call(kernel, name='step', out_shape=(jax.ShapeDtypeStruct((ENC,...  80.2 us
    unnamed x15, local copies, waits for them, and re-layouts  7.7 us

commit v1 on v0

--- a/solution.py
+++ b/solution.py
@@ -20,6 +20,7 @@
 FLOOR = 1e-05
 COUNT = 24576.0
 LAG = 3
+LATE = 4
 
 NN = (((1,), (0,)), ((), ()))
 NT = (((1,), (1,)), ((), ()))
@@ -42,7 +43,7 @@
     x_ref, w1_ref, w2_ref, w3_ref, wd_ref, dec_ref, order_ref, slot_ref, tgt_ref,
     g1_ref, g2_ref, g3_ref, gd_ref, gdec_ref, err_ref,
     w1t, w2t, w3t, wdb, h1s, h2s, feats, lgs, wts, expi, bld, scl, scaled, oh,
-    pfull, prec, zsend, zrecv, lt, lr, lb, br, gbuf, dsall, tmall, wgs, lgrad, b2s,
+    pfull, prec, zsend, zrecv, lt, lr, lb, br, gbuf, dsall, tmall, wgs, lgrad, b2s, b2p,
     decall, esend, elat, epsend, eprec,
     s_ds, r_ds, s_pf, r_pf, s_z, r_z, s_l, r_l, s_b, r_b, s_g, r_g, s_pb, r_pb,
     s_t, r_t, s_d, r_d, s_e, r_e, s_ep, r_ep,
@@ -242,13 +243,13 @@
     targets = []
     decs = []
     for i in range(3):
-        t = jnp.where(chosen, jnp.broadcast_to(tgt_ref[i : i + 1, :][None], shape3), 0.0)
+        t = jnp.where(chosen, jnp.broadcast_to(tgt_ref[i][None], shape3), 0.0)
         targets.append(jnp.sum(t, axis=2, keepdims=True))
         decs.append(
             jnp.where(
                 low,
-                jnp.broadcast_to(dec_ref[i : i + 1, 0:HALF], (8, HALF)),
-                jnp.broadcast_to(dec_ref[i : i + 1, HALF:FEAT], (8, HALF)),
+                jnp.broadcast_to(dec_ref[i, :, 0:HALF], (8, HALF)),
+                jnp.broadcast_to(dec_ref[i, :, HALF:FEAT], (8, HALF)),
             )[None]
         )
 
@@ -316,10 +317,10 @@
         return rc(decall.at[k], decall.at[k], s_d.at[off], r_d.at[k], depth_peer(off), lat)
 
     def send_g(i, c):
-        g_copy(offset_of(i), me).start()
-        return c
-
-    lax.fori_loop(0, K - 1, send_g, 0)
+        g_copy(near_offset_of(i) % K, me).start()
+        return c
+
+    lax.fori_loop(1, K, send_g, 0)
 
     def send_d(off, c):
         d_copy(off, me).start()
@@ -359,7 +360,18 @@
             [jnp.sum(weight_grad[s], axis=0, keepdims=True) for s in range(S)], axis=0
         )
 
+    def third_share(i):
+        d = depth_peer(near_offset_of(i))
+        g3_ref[...] += mm(h2s[d], feats[d], NT)
+        b2p[d] = mm(w3_ref[...], feats[d], NN)
+
+    g3_ref[...] = jnp.zeros_like(g3_ref)
+
     def back_step(i, c):
+        @pl.when(i >= LATE + 1)
+        def _():
+            third_share(i - 1 - LATE)
+
         take_share(i)
 
         @pl.when(i >= 1)
@@ -369,6 +381,7 @@
         return c
 
     lax.fori_loop(0, K, back_step, 0)
+    third_share(K - 1 - LATE)
     back_share(K - 1)
 
     def t_copy(off, k):
@@ -389,8 +402,8 @@
     for k in range(1, K):
         dec_sum = dec_sum + decall[k]
     for i in range(3):
-        gdec_ref[i : i + 1, 0:HALF] = dec_sum[2 * i : 2 * i + 1]
-        gdec_ref[i : i + 1, HALF:FEAT] = dec_sum[2 * i + 1 : 2 * i + 2]
+        gdec_ref[i, :, 0:HALF] = dec_sum[2 * i : 2 * i + 1]
+        gdec_ref[i, :, HALF:FEAT] = dec_sum[2 * i + 1 : 2 * i + 2]
     esend[...] = jnp.broadcast_to(dec_sum[6:7, 0:R], (8, R))
     elat[m] = esend[...]
 
@@ -404,13 +417,11 @@
 
     lax.fori_loop(1, CHIPS, send_e, 0)
 
-    g3_ref[...] = jnp.zeros_like(g3_ref)
-
-    def third_step(d, c):
-        g3_ref[...] += mm(h2s[d], feats[d], NT)
-        return c
-
-    lax.fori_loop(0, K, third_step, 0)
+    def third_step(i, c):
+        third_share(i)
+        return c
+
+    lax.fori_loop(K - LATE, K, third_step, 0)
 
     def wait_e(e, c):
         e_copy(e, (m + e) % CHIPS).wait_recv()
@@ -453,10 +464,9 @@
             [jnp.broadcast_to(lg[s : s + 1, :], (8, R)) for s in range(S)], axis=1
         )
         gdens = gdens + mm(lg8.astype(BF16), h2s[d], NT)
-        b2 = mm(w3_ref[...], feats[d], NN)
         for s in range(S):
             cols = slice(s * R, (s + 1) * R)
-            v = b2[:, cols] + wdb[...] * lg[s : s + 1, :]
+            v = b2p[d, :, cols] + wdb[...] * lg[s : s + 1, :]
             b2s[:, cols] = jnp.where(h2s[d, :, cols].astype(F32) > 0.0, v, 0.0).astype(BF16)
         g2_ref[...] += mm(h1s[d], b2s[...], NT)
         b1 = mm(w2_ref[...], b2s[...], NN)
@@ -498,21 +508,20 @@
     ep_copy.wait_send()
 
 
+def put_out(*refs):
+    for i in range(6):
+        refs[6 + i][...] = refs[i][...]
+
+
 def body(samples, w_first, w_second, w_third, w_density, decoder, depth_order, ray_slot, target):
     vmem = pl.BlockSpec(memory_space=pltpu.VMEM)
     dma = pltpu.SemaphoreType.DMA
     v = pltpu.VMEM
+    results = ((ENC, HID), (HID, HID), (HID, FEAT), (1, HID), (3, 1, FEAT), (1, 1))
     outs = pl.pallas_call(
         kernel,
         name="step",
-        out_shape=(
-            jax.ShapeDtypeStruct((ENC, HID), F32),
-            jax.ShapeDtypeStruct((HID, HID), F32),
-            jax.ShapeDtypeStruct((HID, FEAT), F32),
-            jax.ShapeDtypeStruct((1, HID), F32),
-            jax.ShapeDtypeStruct((3, FEAT), F32),
-            jax.ShapeDtypeStruct((1, 1), F32),
-        ),
+        out_shape=tuple(pltpu.VMEM(shape, F32) for shape in results),
         in_specs=[vmem] * 6 + [pl.BlockSpec(memory_space=pltpu.SMEM)] + [vmem] * 2,
         out_specs=(vmem,) * 6,
         scratch_shapes=[
@@ -544,6 +553,7 @@
             v((K, S, R), F32),
             v((K, S, R), F32),
             v((HID, W), BF16),
+            v((K, HID, W), F32),
             v((K, 8, HALF), F32),
             v((8, R), F32),
             v((CHIPS, 8, R), F32),
@@ -570,17 +580,24 @@
         w_second[0, 0],
         w_third[0, 0],
         w_density[0],
-        decoder[0],
+        jnp.transpose(decoder, (1, 0, 2)),
         depth_order,
         ray_slot,
-        target[0],
+        jnp.transpose(target, (1, 0, 2)),
     )
+    outs = pl.pallas_call(
+        put_out,
+        name="put_out",
+        out_shape=tuple(jax.ShapeDtypeStruct(shape, F32) for shape in results),
+        in_specs=[vmem] * 6,
+        out_specs=(vmem,) * 6,
+    )(*[pltpu.with_memory_space_constraint(o, pltpu.VMEM) for o in outs])
     return (
         outs[0][None, None],
         outs[1][None, None],
         outs[2][None, None],
         outs[3][None],
-        outs[4][None],
+        jnp.transpose(outs[4], (1, 0, 2)),
         outs[5][0, 0],
     )
 

time: 90.6 us -> 76.9 us (0.85)
  local copies, waits for them, and re-layouts: 7.7 us -> 0 us
  Pallas kernels: 80.2 us -> 76 us
  between operations: 2.44 us -> 0.64 us
    unnamed x15 -> x0, local copies, waits for them, and re-layouts: 7.7 us -> none
    pallas_call x1 -> x2, Pallas kernels: 80.2 us -> 76 us  [the longest x1 74.4 us: body(): pl.pallas_call(kernel, name='step', out_shape=tuple((pltpu.VMEM(shape, F3...]
where the time goes in v1:
time: 76.9 us; the launch traced here: 76.6 us
  Pallas kernels  76 us (99%)
    pallas_call x1, Pallas kernels, body(): pl.pallas_call(kernel, name='step', out_shape=tuple((pltpu.VMEM(shape, F3...  74.4 us
    pallas_call x1, Pallas kernels, body(): pl.pallas_call(put_out, name='put_out', out_shape=tuple((jax.ShapeDtypeSt...  1.59 us

profile of v1, /device:TPU:1, one launch (start us, length us, event | category | flops | bytes accessed | tf_op | source)
XLA Modules:
  0.0 76.6 jit_solution(15464950353761455419)
XLA Ops:
  0.6 74.4 %step.1 = (f32[64,256]{1,0:T(8,128)S(1)}, f32[256,256]{1,0:T(8,128)S(1)}, f32[256,512]{1,0:T(8,128)S(1)}, f32[1,256]{1,0:T(1,128)S(1)}, f32[3,1,512]{2,1,0:T(1,128)S(1)}, /*index=5*/f32[1,1]{1,0:T(1,128)}) custom-call(bf16[64,8192]{1,0:T(8,128)(2,1)} %bitcast.13, bf16[64,256]{1,0:T(8,128)(2,1)} %bitcast.16, bf16[256,256]{1,0:T(8,128)(2,1)} %bitcast.15, ...), custom_call_target="tpu_custom_call" | custom-call | tf_op jit(solution)/shard_map/step/pallas_call | solution.py:521
  75.1 1.6 %put_out.1 = (f32[64,256]{1,0:T(8,128)}, f32[256,256]{1,0:T(8,128)}, f32[256,512]{1,0:T(8,128)}, f32[1,256]{1,0:T(1,128)}, f32[3,1,512]{2,1,0:T(1,128)}, /*index=5*/f32[1,1]{1,0:T(1,128)}) custom-call(f32[64,256]{1,0:T(8,128)S(1)} %get-tuple-element.18.refs_0_, f32[256,256]{1,0:T(8,128)S(1)} %get-tuple-element.19.refs_1_, ...), custom_call_target="tpu_custom_call" | custom-call | tf_op jit(solution)/shard_map/put_out/pallas_call | solution.py:588

commit v2 on v1

--- a/solution.py
+++ b/solution.py
@@ -14,13 +14,13 @@
 K = 8
 R = 128
 CHIPS = 16
+G = 8
 W = S * R
 HALF = FEAT // 2
 STEP = 0.04
 FLOOR = 1e-05
 COUNT = 24576.0
-LAG = 3
-LATE = 4
+LATE = 6
 
 NN = (((1,), (0,)), ((), ()))
 NT = (((1,), (1,)), ((), ()))
@@ -43,9 +43,9 @@
     x_ref, w1_ref, w2_ref, w3_ref, wd_ref, dec_ref, order_ref, slot_ref, tgt_ref,
     g1_ref, g2_ref, g3_ref, gd_ref, gdec_ref, err_ref,
     w1t, w2t, w3t, wdb, h1s, h2s, feats, lgs, wts, expi, bld, scl, scaled, oh,
-    pfull, prec, zsend, zrecv, lt, lr, lb, br, gbuf, dsall, tmall, wgs, lgrad, b2s, b2p,
+    pfull, prec, ysend, yrec, zsend, zrecv, lt, lr, lb, br, gbuf, dsall, tmall, wgs, lgrad, b2s, b2p,
     decall, esend, elat, epsend, eprec,
-    s_ds, r_ds, s_pf, r_pf, s_z, r_z, s_l, r_l, s_b, r_b, s_g, r_g, s_pb, r_pb,
+    s_ds, r_ds, s_pf, r_pf, s_y, r_y, s_z, r_z, s_l, r_l, s_b, r_b, s_g, r_g, s_n, r_n, s_pb, r_pb,
     s_t, r_t, s_d, r_d, s_e, r_e, s_ep, r_ep,
 ):
     me = lax.axis_index("depth")
@@ -53,6 +53,12 @@
     h = lat % 2
     m = lat // 2
     sib = lat + 1 - 2 * h
+    g = m // 2
+    st = ((m % 4 + 1) // 2) % 2
+    near = (m + 1 - 2 * (m % 2)) * 2 + h
+
+    def chip_of(s, i):
+        return (i // 2) * 4 + 2 * (i % 2) + (s + i) % 2
 
     def depth_peer(off):
         return (me + off) % K
@@ -124,7 +130,7 @@
     lax.fori_loop(1, K, send_ds, 0)
 
     row = lax.broadcasted_iota(jnp.int32, (2 * R, R), 0)
-    code = (((row // 8) % CHIPS) * 2 + row // R) * 4 + row % 4
+    code = (chip_of((row // 64) % 2, (row // 8) % G) * 2 + row // R) * 4 + row % 4
     code_lo = jnp.where((row // 4) % 2 == 0, code, -1)
     code_hi = jnp.where((row // 4) % 2 == 1, code, -1)
 
@@ -178,40 +184,51 @@
     def pf_copy(d):
         return rc(pfull.at[d, 1 - h], prec.at[d], s_pf.at[d], r_pf.at[d], me, sib)
 
+    def y_copy(d):
+        return rc(ysend.at[d], yrec.at[d], s_y.at[d], r_y.at[d], me, near)
+
     def z_copy(d, k):
         return rc(zsend.at[d], zrecv.at[k], s_z.at[d], r_z.at[k], d, lat)
 
-    def make_scaled(d):
+    def make_scaled(i, c):
+        d = depth_peer(offset_of(i))
         sc = scl[pl.ds(d, 1), :]
         sc = jnp.concatenate([sc, sc], axis=1)
         scaled[d] = (bld[d] * sc).astype(BF16)
         placed = mm(oh[d], scaled[d], NT).astype(BF16)
-        pfull[d, 0] = placed[0:R]
-        pfull[d, 1] = placed[R : 2 * R]
+        for half in range(2):
+            for s in range(2):
+                r0 = half * R + s * 64
+                pfull[d, half, s] = placed[r0 : r0 + 64]
         pf_copy(d).start()
-
-    def pair_sum(d):
+        return c
+
+    lax.fori_loop(0, K, make_scaled, 0)
+
+    def pair_sum(d, s):
+        return pfull[d, h, s].astype(F32) + prec[d, s].astype(F32)
+
+    def send_near(i, c):
+        d = depth_peer(offset_of(i))
         pf_copy(d).wait_recv()
-        return (pfull[d, h].astype(F32) + prec[d].astype(F32)).astype(BF16)
-
-    def send_share(i):
+        ysend[d] = pair_sum(d, 1 - st).astype(BF16)
+        y_copy(d).start()
+        return c
+
+    lax.fori_loop(0, K, send_near, 0)
+
+    def group_sum(d):
+        y_copy(d).wait_recv()
+        return (pair_sum(d, st) + yrec[d].astype(F32)).astype(BF16)
+
+    def send_share(i, c):
         d = depth_peer(offset_of(i))
-        zsend[d] = pair_sum(d)
+        zsend[d] = group_sum(d)
         z_copy(d, me).start()
-
-    def scaled_step(i, c):
-        make_scaled(depth_peer(offset_of(i)))
-
-        @pl.when(i >= LAG)
-        def _():
-            send_share(i - LAG)
-
-        return c
-
-    lax.fori_loop(0, K, scaled_step, 0)
-    for i in range(K - LAG, K - 1):
-        send_share(i)
-    zrecv[me] = pair_sum(me)
+        return c
+
+    lax.fori_loop(0, K - 1, send_share, 0)
+    zrecv[me] = group_sum(me)
 
     def wait_z(off, c):
         z_copy(me, depth_peer(off)).wait_recv()
@@ -221,18 +238,18 @@
     total = zrecv[0].astype(F32)
     for k in range(1, K):
         total = total + zrecv[k].astype(F32)
-    lt[...] = total.reshape(CHIPS, 8, HALF)
+    lt[...] = total.reshape(G, 8, HALF)
 
     def l_copy(e, src):
-        to = (m + e) % CHIPS
-        return rc(lt.at[to], lr.at[src], s_l.at[to], r_l.at[src], me, to * 2 + h)
+        to = (g + e) % G
+        return rc(lt.at[to], lr.at[src], s_l.at[to], r_l.at[src], me, chip_of(st, to) * 2 + h)
 
     def send_l(e, c):
-        l_copy(e, m).start()
-        return c
-
-    lax.fori_loop(1, CHIPS, send_l, 0)
-    lr[m] = lt[m]
+        l_copy(e, g).start()
+        return c
+
+    lax.fori_loop(1, G, send_l, 0)
+    lr[g] = lt[g]
 
     shape3 = (8, 8, 32)
     grp = lax.broadcasted_iota(jnp.int32, shape3, 0)
@@ -261,12 +278,11 @@
         return jnp.concatenate([v, v], axis=2)
 
     def wait_l(e, c):
-        l_copy(e, (m + e) % CHIPS).wait_recv()
-        return c
-
-    lax.fori_loop(1, CHIPS, wait_l, 0)
-    arrived = lr[...].reshape(8, 2, 8, HALF)
-    mean = (arrived[:, 0] + arrived[:, 1]) * 0.25
+        l_copy(e, (g + e) % G).wait_recv()
+        return c
+
+    lax.fori_loop(1, G, wait_l, 0)
+    mean = lr[...] * 0.25
     inverse = wide(lax.rsqrt(both_halves(mean * mean) * (1.0 / FEAT) + FLOOR))
     normed = mean * inverse
     normed_grad = jnp.zeros((8, 8, HALF), F32)
@@ -285,15 +301,15 @@
     lb[...] = pixel_grad.astype(BF16).astype(F32)
 
     def b_copy(e, src):
-        to = (m + e) % CHIPS
-        return rc(lb.at[to // 2], br.at[src], s_b.at[to], r_b.at[src], me, to * 2 + h)
+        to = (g + e) % G
+        return rc(lb.at[to], br.at[src], s_b.at[to], r_b.at[src], me, chip_of(st, to) * 2 + h)
 
     def send_b(e, c):
-        b_copy(e, m).start()
-        return c
-
-    lax.fori_loop(1, CHIPS, send_b, 0)
-    br[m] = lb[m // 2]
+        b_copy(e, g).start()
+        return c
+
+    lax.fori_loop(1, G, send_b, 0)
+    br[g] = lb[g]
 
     err_row = jnp.sum(jnp.sum(square, axis=0), axis=0, keepdims=True) * 0.5
     dec_rows.append(jnp.concatenate([err_row, err_row], axis=1))
@@ -301,14 +317,19 @@
     decall[me] = jnp.concatenate(dec_rows, axis=0)
 
     def wait_b(e, c):
-        b_copy(e, (m + e) % CHIPS).wait_recv()
-        return c
-
-    lax.fori_loop(1, CHIPS, wait_b, 0)
-    gbuf[me, h] = br[...].reshape(R, HALF).astype(BF16)
+        b_copy(e, (g + e) % G).wait_recv()
+        return c
+
+    lax.fori_loop(1, G, wait_b, 0)
+    gbuf[me, h, st] = br[...].reshape(R // 2, HALF).astype(BF16)
 
     def g_copy(off, k):
-        return rc(gbuf.at[k, h], gbuf.at[k, h], s_g.at[off], r_g.at[k], depth_peer(off), lat)
+        ref = gbuf.at[k, h, st]
+        return rc(ref, ref, s_g.at[off], r_g.at[k], depth_peer(off), lat)
+
+    def n_copy(d, s):
+        ref = gbuf.at[d, h, s]
+        return rc(ref, ref, s_n.at[d], r_n.at[d], me, near)
 
     def pb_copy(d, half):
         return rc(gbuf.at[d, half], gbuf.at[d, half], s_pb.at[d], r_pb.at[d], me, sib)
@@ -335,6 +356,11 @@
         def _():
             g_copy(near_offset_of(i) % K, d).wait_recv()
 
+        n_copy(d, st).start()
+
+    def pass_share(i):
+        d = depth_peer(near_offset_of(i))
+        n_copy(d, 1 - st).wait_recv()
         pb_copy(d, h).start()
 
     def back_share(i):
@@ -376,12 +402,18 @@
 
         @pl.when(i >= 1)
         def _():
-            back_share(i - 1)
+            pass_share(i - 1)
+
+        @pl.when(i >= 2)
+        def _():
+            back_share(i - 2)
 
         return c
 
     lax.fori_loop(0, K, back_step, 0)
     third_share(K - 1 - LATE)
+    pass_share(K - 1)
+    back_share(K - 2)
     back_share(K - 1)
 
     def t_copy(off, k):
@@ -422,18 +454,6 @@
         return c
 
     lax.fori_loop(K - LATE, K, third_step, 0)
-
-    def wait_e(e, c):
-        e_copy(e, (m + e) % CHIPS).wait_recv()
-        return c
-
-    lax.fori_loop(1, CHIPS, wait_e, 0)
-    err_sum = elat[0]
-    for k in range(1, CHIPS):
-        err_sum = err_sum + elat[k]
-    epsend[...] = err_sum
-    ep_copy = rc(epsend, eprec, s_ep, r_ep, me, sib)
-    ep_copy.start()
 
     def wait_t(off, c):
         t_copy(off, depth_peer(off)).wait_recv()
@@ -455,6 +475,18 @@
         sig = 1.0 / (1.0 + jnp.exp(-lg))
         lgrad[d] = (density_grad * sig).astype(BF16).astype(F32)
 
+    def wait_e(e, c):
+        e_copy(e, (m + e) % CHIPS).wait_recv()
+        return c
+
+    lax.fori_loop(1, CHIPS, wait_e, 0)
+    err_sum = elat[0]
+    for k in range(1, CHIPS):
+        err_sum = err_sum + elat[k]
+    epsend[...] = err_sum
+    ep_copy = rc(epsend, eprec, s_ep, r_ep, me, sib)
+    ep_copy.start()
+
     g1_ref[...] = jnp.zeros_like(g1_ref)
     g2_ref[...] = jnp.zeros_like(g2_ref)
 
@@ -487,13 +519,13 @@
         g_copy(off, me).wait_send()
         d_copy(off, me).wait_send()
         t_copy(off, me).wait_send()
+        l_copy(off, g).wait_send()
+        b_copy(off, g).wait_send()
         return c
 
     lax.fori_loop(1, K, end_depth, 0)
 
     def end_lateral(e, c):
-        l_copy(e, m).wait_send()
-        b_copy(e, m).wait_send()
         e_copy(e, m).wait_send()
         return c
 
@@ -501,6 +533,8 @@
 
     def end_pair(d, c):
         pf_copy(d).wait_send()
+        y_copy(d).wait_send()
+        n_copy(d, st).wait_send()
         pb_copy(d, h).wait_send()
         return c
 
@@ -539,15 +573,17 @@
             v((K, R), F32),
             v((K, HALF, 2 * R), BF16),
             v((K, 2 * R, 2 * R), BF16),
-            v((K, 2, R, HALF), BF16),
-            v((K, R, HALF), BF16),
-            v((K, R, HALF), BF16),
-            v((K, R, HALF), BF16),
-            v((CHIPS, 8, HALF), F32),
-            v((CHIPS, 8, HALF), F32),
-            v((8, 8, HALF), F32),
-            v((CHIPS, 8, HALF), F32),
-            v((K, 2, R, HALF), BF16),
+            v((K, 2, 2, R // 2, HALF), BF16),
+            v((K, 2, R // 2, HALF), BF16),
+            v((K, R // 2, HALF), BF16),
+            v((K, R // 2, HALF), BF16),
+            v((K, R // 2, HALF), BF16),
+            v((K, R // 2, HALF), BF16),
+            v((G, 8, HALF), F32),
+            v((G, 8, HALF), F32),
+            v((G, 8, HALF), F32),
+            v((G, 8, HALF), F32),
+            v((K, 2, 2, R // 2, HALF), BF16),
             v((K, K, R), F32),
             v((K, K, R), F32),
             v((K, S, R), F32),
@@ -562,8 +598,10 @@
             dma((K,)), dma((K,)),
             dma((K,)), dma((K,)),
             dma((K,)), dma((K,)),
-            dma((CHIPS,)), dma((CHIPS,)),
-            dma((CHIPS,)), dma((CHIPS,)),
+            dma((K,)), dma((K,)),
+            dma((G,)), dma((G,)),
+            dma((G,)), dma((G,)),
+            dma((K,)), dma((K,)),
             dma((K,)), dma((K,)),
             dma((K,)), dma((K,)),
             dma((K,)), dma((K,)),

time: 76.9 us -> 76.3 us (level)
  no operation moved by 1% of the time
where the time goes in v2:
time: 76.3 us; the launch traced here: 76.2 us
  Pallas kernels  75.6 us (99%)
    pallas_call x1, Pallas kernels, body(): pl.pallas_call(kernel, name='step', out_shape=tuple((pltpu.VMEM(shape, F3...  74 us
    pallas_call x1, Pallas kernels, body(): pl.pallas_call(put_out, name='put_out', out_shape=tuple((jax.ShapeDtypeSt...  1.59 us

profile of v2, /device:TPU:1, one launch (start us, length us, event | category | flops | bytes accessed | tf_op | source)
XLA Modules:
  0.0 76.2 jit_solution(5664814052303181927)
XLA Ops:
  0.6 74.0 %step.1 = (f32[64,256]{1,0:T(8,128)S(1)}, f32[256,256]{1,0:T(8,128)S(1)}, f32[256,512]{1,0:T(8,128)S(1)}, f32[1,256]{1,0:T(1,128)S(1)}, f32[3,1,512]{2,1,0:T(1,128)S(1)}, /*index=5*/f32[1,1]{1,0:T(1,128)}) custom-call(bf16[64,8192]{1,0:T(8,128)(2,1)} %bitcast.13, bf16[64,256]{1,0:T(8,128)(2,1)} %bitcast.16, bf16[256,256]{1,0:T(8,128)(2,1)} %bitcast.15, ...), custom_call_target="tpu_custom_call" | custom-call | tf_op jit(solution)/shard_map/step/pallas_call | solution.py:555
  74.6 1.6 %put_out.1 = (f32[64,256]{1,0:T(8,128)}, f32[256,256]{1,0:T(8,128)}, f32[256,512]{1,0:T(8,128)}, f32[1,256]{1,0:T(1,128)}, f32[3,1,512]{2,1,0:T(1,128)}, /*index=5*/f32[1,1]{1,0:T(1,128)}) custom-call(f32[64,256]{1,0:T(8,128)S(1)} %get-tuple-element.18.refs_0_, f32[256,256]{1,0:T(8,128)S(1)} %get-tuple-element.19.refs_1_, ...), custom_call_target="tpu_custom_call" | custom-call | tf_op jit(solution)/shard_map/put_out/pallas_call | solution.py:626

commit v3 on v2

--- a/solution.py
+++ b/solution.py
@@ -20,7 +20,8 @@
 STEP = 0.04
 FLOOR = 1e-05
 COUNT = 24576.0
-LATE = 6
+NEAR_LAG = 3
+PAIR_LAG = 5
 
 NN = (((1,), (0,)), ((), ()))
 NT = (((1,), (1,)), ((), ()))
@@ -42,10 +43,10 @@
 def kernel(
     x_ref, w1_ref, w2_ref, w3_ref, wd_ref, dec_ref, order_ref, slot_ref, tgt_ref,
     g1_ref, g2_ref, g3_ref, gd_ref, gdec_ref, err_ref,
-    w1t, w2t, w3t, wdb, h1s, h2s, feats, lgs, wts, expi, bld, scl, scaled, oh,
+    xs, w1t, w2t, w3t, wdb, h1s, h2s, feats, lgs, wts, expi, bld, scl, scaled, oh,
     pfull, prec, ysend, yrec, zsend, zrecv, lt, lr, lb, br, gbuf, dsall, tmall, wgs, lgrad, b2s, b2p,
     decall, esend, elat, epsend, eprec,
-    s_ds, r_ds, s_pf, r_pf, s_y, r_y, s_z, r_z, s_l, r_l, s_b, r_b, s_g, r_g, s_n, r_n, s_pb, r_pb,
+    s_x, s_ds, r_ds, s_pf, r_pf, s_y, r_y, s_z, r_z, s_l, r_l, s_b, r_b, s_g, r_g, s_n, r_n, s_pb, r_pb,
     s_t, r_t, s_d, r_d, s_e, r_e, s_ep, r_ep,
 ):
     me = lax.axis_index("depth")
@@ -69,6 +70,13 @@
             device_id=(z, l), device_id_type=MESH,
         )
 
+    def x_copy(s):
+        cols = pl.ds(pl.multiple_of(s * (K * R), K * R), K * R)
+        return pltpu.make_async_copy(x_ref.at[:, cols], xs.at[s], s_x.at[s])
+
+    for s in range(S):
+        x_copy(s).start()
+
     barrier = pltpu.get_barrier_semaphore()
 
     def greet_depth(e, c):
@@ -87,26 +95,28 @@
 
     w1t[...] = w1_ref[...].T
     w2t[...] = w2_ref[...].T
-    w3t[...] = w3_ref[...].T
     wd8 = jnp.broadcast_to(wd_ref[...], (8, HID))
     wdb[...] = jnp.broadcast_to(wd_ref[...].astype(F32), (R, HID)).T
 
     def take_x(d):
         return jnp.concatenate(
-            [x_ref[:, pl.ds(pl.multiple_of(s * (K * R) + d * R, R), R)] for s in range(S)], axis=1
+            [xs[s, :, pl.ds(pl.multiple_of(d * R, R), R)] for s in range(S)], axis=1
         )
 
-    def first_pass(d, c):
-        x = take_x(d)
-        h1s[d] = jnp.maximum(mm(w1t[...], x, NN), 0.0).astype(BF16)
-        h2s[d] = jnp.maximum(mm(w2t[...], h1s[d], NN), 0.0).astype(BF16)
-        lg = mm(wd8, h2s[d], NN)
-        lgs[d] = jnp.concatenate(
-            [lg[s : s + 1, s * R : (s + 1) * R] for s in range(S)], axis=0
-        )
-        return c
-
-    lax.fori_loop(0, K, first_pass, 0)
+    def first_pass(s, c):
+        x_copy(s).wait()
+        cols = pl.ds(pl.multiple_of(s * R, R), R)
+        h1 = jnp.maximum(mm(w1t[...], xs[s], NN), 0.0).astype(BF16)
+        h2 = jnp.maximum(mm(w2t[...], h1, NN), 0.0).astype(BF16)
+        lg = mm(wd8, h2, NN)
+        for d in range(K):
+            here = slice(d * R, (d + 1) * R)
+            h1s[d, :, cols] = h1[:, here]
+            h2s[d, :, cols] = h2[:, here]
+            lgs[d, pl.ds(s, 1), :] = lg[0:1, here]
+        return c
+
+    lax.fori_loop(0, S, first_pass, 0)
 
     sub = lax.broadcasted_iota(jnp.int32, (K, S, R), 1)
     logits = lgs[...]
@@ -128,6 +138,7 @@
         return c
 
     lax.fori_loop(1, K, send_ds, 0)
+    w3t[...] = w3_ref[...].T
 
     row = lax.broadcasted_iota(jnp.int32, (2 * R, R), 0)
     code = (chip_of((row // 64) % 2, (row // 8) % G) * 2 + row // R) * 4 + row % 4
@@ -386,35 +397,22 @@
             [jnp.sum(weight_grad[s], axis=0, keepdims=True) for s in range(S)], axis=0
         )
 
-    def third_share(i):
-        d = depth_peer(near_offset_of(i))
-        g3_ref[...] += mm(h2s[d], feats[d], NT)
-        b2p[d] = mm(w3_ref[...], feats[d], NN)
-
-    g3_ref[...] = jnp.zeros_like(g3_ref)
-
     def back_step(i, c):
-        @pl.when(i >= LATE + 1)
+        @pl.when(i < K)
         def _():
-            third_share(i - 1 - LATE)
-
-        take_share(i)
-
-        @pl.when(i >= 1)
+            take_share(i)
+
+        @pl.when((i >= NEAR_LAG) & (i < K + NEAR_LAG))
         def _():
-            pass_share(i - 1)
-
-        @pl.when(i >= 2)
+            pass_share(i - NEAR_LAG)
+
+        @pl.when(i >= PAIR_LAG)
         def _():
-            back_share(i - 2)
-
-        return c
-
-    lax.fori_loop(0, K, back_step, 0)
-    third_share(K - 1 - LATE)
-    pass_share(K - 1)
-    back_share(K - 2)
-    back_share(K - 1)
+            back_share(i - PAIR_LAG)
+
+        return c
+
+    lax.fori_loop(0, K + PAIR_LAG, back_step, 0)
 
     def t_copy(off, k):
         return rc(tmall.at[k], tmall.at[k], s_t.at[off], r_t.at[k], depth_peer(off), lat)
@@ -449,11 +447,14 @@
 
     lax.fori_loop(1, CHIPS, send_e, 0)
 
-    def third_step(i, c):
-        third_share(i)
-        return c
-
-    lax.fori_loop(K - LATE, K, third_step, 0)
+    g3_ref[...] = jnp.zeros_like(g3_ref)
+
+    def third_step(d, c):
+        g3_ref[...] += mm(h2s[d], feats[d], NT)
+        b2p[d] = mm(w3_ref[...], feats[d], NN)
+        return c
+
+    lax.fori_loop(0, K, third_step, 0)
 
     def wait_t(off, c):
         t_copy(off, depth_peer(off)).wait_recv()
@@ -556,9 +557,10 @@
         kernel,
         name="step",
         out_shape=tuple(pltpu.VMEM(shape, F32) for shape in results),
-        in_specs=[vmem] * 6 + [pl.BlockSpec(memory_space=pltpu.SMEM)] + [vmem] * 2,
+        in_specs=[pl.BlockSpec(memory_space=pl.ANY)] + [vmem] * 5 + [pl.BlockSpec(memory_space=pltpu.SMEM)] + [vmem] * 2,
         out_specs=(vmem,) * 6,
         scratch_shapes=[
+            v((S, ENC, K * R), BF16),
             v((HID, ENC), BF16),
             v((HID, HID), BF16),
             v((FEAT, HID), BF16),
@@ -595,6 +597,7 @@
             v((CHIPS, 8, R), F32),
             v((8, R), F32),
             v((8, R), F32),
+            dma((S,)),
             dma((K,)), dma((K,)),
             dma((K,)), dma((K,)),
             dma((K,)), dma((K,)),

time: 76.3 us -> 71.8 us (0.941)
  Pallas kernels: 75.6 us -> 71 us
    pallas_call x1, Pallas kernels: 74 us -> 69.4 us  [body(): pl.pallas_call(kernel, name='step', out_shape=tuple((pltpu.VMEM(shape, F3...]
where the time goes in v3:
time: 71.8 us; the launch traced here: 71.7 us
  Pallas kernels  71 us (99%)
    pallas_call x1, Pallas kernels, body(): pl.pallas_call(kernel, name='step', out_shape=tuple((pltpu.VMEM(shape, F3...  69.4 us
    pallas_call x1, Pallas kernels, body(): pl.pallas_call(put_out, name='put_out', out_shape=tuple((jax.ShapeDtypeSt...  1.59 us

profile of v3, /device:TPU:1, one launch (start us, length us, event | category | flops | bytes accessed | tf_op | source)
XLA Modules:
  0.0 71.7 jit_solution(18205595003785465191)
XLA Ops:
  0.6 69.4 %step.1 = (f32[64,256]{1,0:T(8,128)S(1)}, f32[256,256]{1,0:T(8,128)S(1)}, f32[256,512]{1,0:T(8,128)S(1)}, f32[1,256]{1,0:T(1,128)S(1)}, f32[3,1,512]{2,1,0:T(1,128)S(1)}, /*index=5*/f32[1,1]{1,0:T(1,128)}) custom-call(bf16[64,8192]{1,0:T(8,128)(2,1)} %bitcast.13, bf16[64,256]{1,0:T(8,128)(2,1)} %bitcast.16, bf16[256,256]{1,0:T(8,128)(2,1)} %bitcast.15, ...), custom_call_target="tpu_custom_call" | custom-call | tf_op jit(solution)/shard_map/step/pallas_call | solution.py:556
  70.1 1.6 %put_out.1 = (f32[64,256]{1,0:T(8,128)}, f32[256,256]{1,0:T(8,128)}, f32[256,512]{1,0:T(8,128)}, f32[1,256]{1,0:T(1,128)}, f32[3,1,512]{2,1,0:T(1,128)}, /*index=5*/f32[1,1]{1,0:T(1,128)}) custom-call(f32[64,256]{1,0:T(8,128)S(1)} %get-tuple-element.18.refs_0_, f32[256,256]{1,0:T(8,128)S(1)} %get-tuple-element.19.refs_1_, ...), custom_call_target="tpu_custom_call" | custom-call | tf_op jit(solution)/shard_map/put_out/pallas_call | solution.py:629

commit v4 on v3

--- a/solution.py
+++ b/solution.py
@@ -20,8 +20,9 @@
 STEP = 0.04
 FLOOR = 1e-05
 COUNT = 24576.0
-NEAR_LAG = 3
-PAIR_LAG = 5
+NEAR_LAG = 4
+PAIR_LAG = 7
+FIRST = 3
 
 NN = (((1,), (0,)), ((), ()))
 NT = (((1,), (1,)), ((), ()))
@@ -44,7 +45,7 @@
     x_ref, w1_ref, w2_ref, w3_ref, wd_ref, dec_ref, order_ref, slot_ref, tgt_ref,
     g1_ref, g2_ref, g3_ref, gd_ref, gdec_ref, err_ref,
     xs, w1t, w2t, w3t, wdb, h1s, h2s, feats, lgs, wts, expi, bld, scl, scaled, oh,
-    pfull, prec, ysend, yrec, zsend, zrecv, lt, lr, lb, br, gbuf, dsall, tmall, wgs, lgrad, b2s, b2p,
+    pfull, prec, ysend, yrec, zsend, zrecv, lt, lr, lb, br, gbuf, dsall, tmall, wgs, lgrad, b2s, b2t, b2p,
     decall, esend, elat, epsend, eprec,
     s_x, s_ds, r_ds, s_pf, r_pf, s_y, r_y, s_z, r_z, s_l, r_l, s_b, r_b, s_g, r_g, s_n, r_n, s_pb, r_pb,
     s_t, r_t, s_d, r_d, s_e, r_e, s_ep, r_ep,
@@ -106,8 +107,8 @@
     def first_pass(s, c):
         x_copy(s).wait()
         cols = pl.ds(pl.multiple_of(s * R, R), R)
-        h1 = jnp.maximum(mm(w1t[...], xs[s], NN), 0.0).astype(BF16)
-        h2 = jnp.maximum(mm(w2t[...], h1, NN), 0.0).astype(BF16)
+        h1 = jnp.maximum(mm(w1t[...], xs[s], NN).astype(BF16), 0)
+        h2 = jnp.maximum(mm(w2t[...], h1, NN).astype(BF16), 0)
         lg = mm(wd8, h2, NN)
         for d in range(K):
             here = slice(d * R, (d + 1) * R)
@@ -397,18 +398,28 @@
             [jnp.sum(weight_grad[s], axis=0, keepdims=True) for s in range(S)], axis=0
         )
 
+    def third_share(d):
+        g3_ref[...] += mm(h2s[d], feats[d], NT)
+        b2p[d] = mm(w3_ref[...], feats[d], NN)
+
+    g3_ref[...] = jnp.zeros_like(g3_ref)
+
     def back_step(i, c):
+        @pl.when((i == FIRST) | (i > PAIR_LAG))
+        def _():
+            back_share(jnp.where(i == FIRST, 0, i - PAIR_LAG))
+
+        @pl.when(i == FIRST + 1)
+        def _():
+            third_share(me)
+
         @pl.when(i < K)
         def _():
             take_share(i)
 
-        @pl.when((i >= NEAR_LAG) & (i < K + NEAR_LAG))
+        @pl.when((i == 0) | ((i > NEAR_LAG) & (i < K + NEAR_LAG)))
         def _():
-            pass_share(i - NEAR_LAG)
-
-        @pl.when(i >= PAIR_LAG)
-        def _():
-            back_share(i - PAIR_LAG)
+            pass_share(jnp.where(i == 0, 0, i - NEAR_LAG))
 
         return c
 
@@ -447,14 +458,11 @@
 
     lax.fori_loop(1, CHIPS, send_e, 0)
 
-    g3_ref[...] = jnp.zeros_like(g3_ref)
-
-    def third_step(d, c):
-        g3_ref[...] += mm(h2s[d], feats[d], NT)
-        b2p[d] = mm(w3_ref[...], feats[d], NN)
-        return c
-
-    lax.fori_loop(0, K, third_step, 0)
+    def third_step(i, c):
+        third_share(depth_peer(i))
+        return c
+
+    lax.fori_loop(1, K, third_step, 0)
 
     def wait_t(off, c):
         t_copy(off, depth_peer(off)).wait_recv()
@@ -491,23 +499,33 @@
     g1_ref[...] = jnp.zeros_like(g1_ref)
     g2_ref[...] = jnp.zeros_like(g2_ref)
 
-    def last_step(d, gdens):
+    def masked_back_two(d, out):
         lg = lgrad[d]
         lg8 = jnp.concatenate(
             [jnp.broadcast_to(lg[s : s + 1, :], (8, R)) for s in range(S)], axis=1
         )
-        gdens = gdens + mm(lg8.astype(BF16), h2s[d], NT)
         for s in range(S):
             cols = slice(s * R, (s + 1) * R)
             v = b2p[d, :, cols] + wdb[...] * lg[s : s + 1, :]
-            b2s[:, cols] = jnp.where(h2s[d, :, cols].astype(F32) > 0.0, v, 0.0).astype(BF16)
-        g2_ref[...] += mm(h1s[d], b2s[...], NT)
-        b1 = mm(w2_ref[...], b2s[...], NN)
-        b1 = jnp.where(h1s[d].astype(F32) > 0.0, b1, 0.0).astype(BF16)
-        g1_ref[...] += mm(take_x(d), b1, NT)
+            out[:, cols] = jnp.where(
+                h2s[d, :, cols] > 0, v.astype(BF16), jnp.zeros_like(v, BF16)
+            )
+        return mm(lg8.astype(BF16), h2s[d], NT)
+
+    def masked_back_one(d, b2):
+        b1 = mm(w2_ref[...], b2[...], NN).astype(BF16)
+        return jnp.where(h1s[d] > 0, b1, jnp.zeros_like(b1))
+
+    def last_step(i, gdens):
+        d, e = 2 * i, 2 * i + 1
+        gdens = gdens + masked_back_two(d, b2s) + masked_back_two(e, b2t)
+        b1s = masked_back_one(d, b2s)
+        b1t = masked_back_one(e, b2t)
+        g2_ref[...] += mm(h1s[d], b2s[...], NT) + mm(h1s[e], b2t[...], NT)
+        g1_ref[...] += mm(take_x(d), b1s, NT) + mm(take_x(e), b1t, NT)
         return gdens
 
-    gdens = lax.fori_loop(0, K, last_step, jnp.zeros((8, HID), F32))
+    gdens = lax.fori_loop(0, K // 2, last_step, jnp.zeros((8, HID), F32))
     gd_ref[...] = gdens[0:1]
 
     ep_copy.wait_recv()
@@ -591,6 +609,7 @@
             v((K, S, R), F32),
             v((K, S, R), F32),
             v((HID, W), BF16),
+            v((HID, W), BF16),
             v((K, HID, W), F32),
             v((K, 8, HALF), F32),
             v((8, R), F32),

time: 71.8 us -> 70.4 us (0.981)
  Pallas kernels: 71 us -> 69.6 us
    pallas_call x1, Pallas kernels: 69.4 us -> 68 us  [body(): pl.pallas_call(kernel, name='step', out_shape=tuple((pltpu.VMEM(shape, F3...]
where the time goes in v4:
time: 70.4 us; the launch traced here: 70.2 us
  Pallas kernels  69.6 us (99%)
    pallas_call x1, Pallas kernels, body(): pl.pallas_call(kernel, name='step', out_shape=tuple((pltpu.VMEM(shape, F3...  68 us
    pallas_call x1, Pallas kernels, body(): pl.pallas_call(put_out, name='put_out', out_shape=tuple((jax.ShapeDtypeSt...  1.59 us

profile of v4, /device:TPU:1, one launch (start us, length us, event | category | flops | bytes accessed | tf_op | source)
XLA Modules:
  0.0 70.2 jit_solution(8393306054083393858)
XLA Ops:
  0.6 68.0 %step.1 = (f32[64,256]{1,0:T(8,128)S(1)}, f32[256,256]{1,0:T(8,128)S(1)}, f32[256,512]{1,0:T(8,128)S(1)}, f32[1,256]{1,0:T(1,128)S(1)}, f32[3,1,512]{2,1,0:T(1,128)S(1)}, /*index=5*/f32[1,1]{1,0:T(1,128)}) custom-call(bf16[64,8192]{1,0:T(8,128)(2,1)} %bitcast.13, bf16[64,256]{1,0:T(8,128)(2,1)} %bitcast.16, bf16[256,256]{1,0:T(8,128)(2,1)} %bitcast.15, ...), custom_call_target="tpu_custom_call" | custom-call | tf_op jit(solution)/shard_map/step/pallas_call | solution.py:574
  68.6 1.6 %put_out.1 = (f32[64,256]{1,0:T(8,128)}, f32[256,256]{1,0:T(8,128)}, f32[256,512]{1,0:T(8,128)}, f32[1,256]{1,0:T(1,128)}, f32[3,1,512]{2,1,0:T(1,128)}, /*index=5*/f32[1,1]{1,0:T(1,128)}) custom-call(f32[64,256]{1,0:T(8,128)S(1)} %get-tuple-element.18.refs_0_, f32[256,256]{1,0:T(8,128)S(1)} %get-tuple-element.19.refs_1_, ...), custom_call_target="tpu_custom_call" | custom-call | tf_op jit(solution)/shard_map/put_out/pallas_call | solution.py:648

commit v5 on v4

--- a/solution.py
+++ b/solution.py
@@ -78,6 +78,10 @@
     for s in range(S):
         x_copy(s).start()
 
+    def blocks(ref, n, ssem, rsem):
+        part = ref.at[pl.ds(0, n)]
+        return rc(part, part, ssem, rsem, depth_peer(1), lat)
+
     barrier = pltpu.get_barrier_semaphore()
 
     def greet_depth(e, c):
@@ -132,7 +136,7 @@
     pl.semaphore_wait(barrier, K - 1 + CHIPS - 1 + 1)
 
     def ds_copy(off, k):
-        return rc(dsall.at[k], dsall.at[k], s_ds.at[off], r_ds.at[k], depth_peer(off), lat)
+        return rc(dsall.at[k], dsall.at[k], s_ds, r_ds, depth_peer(off), lat)
 
     def send_ds(off, c):
         ds_copy(off, me).start()
@@ -183,24 +187,20 @@
     for p in range(K):
         mine = mine + jnp.where(order_ref[0, p] == me, p, 0)
 
-    def wait_ds(off, c):
-        ds_copy(off, depth_peer(off)).wait_recv()
-        return c
-
-    lax.fori_loop(1, K, wait_ds, 0)
+    blocks(dsall, K - 1, s_ds, r_ds).wait_recv()
     before = jnp.zeros((K, R), F32)
     for k in range(K):
         before = before + dsall[k] * jnp.where(places[k] < mine, 1.0, 0.0)
     scl[...] = jnp.exp(-before)
 
     def pf_copy(d):
-        return rc(pfull.at[d, 1 - h], prec.at[d], s_pf.at[d], r_pf.at[d], me, sib)
+        return rc(pfull.at[d, 1 - h], prec.at[d], s_pf, r_pf.at[d], me, sib)
 
     def y_copy(d):
-        return rc(ysend.at[d], yrec.at[d], s_y.at[d], r_y.at[d], me, near)
+        return rc(ysend.at[d], yrec.at[d], s_y, r_y.at[d], me, near)
 
     def z_copy(d, k):
-        return rc(zsend.at[d], zrecv.at[k], s_z.at[d], r_z.at[k], d, lat)
+        return rc(zsend.at[d], zrecv.at[k], s_z, r_z, d, lat)
 
     def make_scaled(i, c):
         d = depth_peer(offset_of(i))
@@ -242,11 +242,7 @@
     lax.fori_loop(0, K - 1, send_share, 0)
     zrecv[me] = group_sum(me)
 
-    def wait_z(off, c):
-        z_copy(me, depth_peer(off)).wait_recv()
-        return c
-
-    lax.fori_loop(1, K, wait_z, 0)
+    blocks(zrecv, K - 1, s_z, r_z).wait_recv()
     total = zrecv[0].astype(F32)
     for k in range(1, K):
         total = total + zrecv[k].astype(F32)
@@ -254,7 +250,7 @@
 
     def l_copy(e, src):
         to = (g + e) % G
-        return rc(lt.at[to], lr.at[src], s_l.at[to], r_l.at[src], me, chip_of(st, to) * 2 + h)
+        return rc(lt.at[to], lr.at[src], s_l, r_l, me, chip_of(st, to) * 2 + h)
 
     def send_l(e, c):
         l_copy(e, g).start()
@@ -289,11 +285,7 @@
     def wide(v):
         return jnp.concatenate([v, v], axis=2)
 
-    def wait_l(e, c):
-        l_copy(e, (g + e) % G).wait_recv()
-        return c
-
-    lax.fori_loop(1, G, wait_l, 0)
+    blocks(lr, G - 1, s_l, r_l).wait_recv()
     mean = lr[...] * 0.25
     inverse = wide(lax.rsqrt(both_halves(mean * mean) * (1.0 / FEAT) + FLOOR))
     normed = mean * inverse
@@ -314,7 +306,7 @@
 
     def b_copy(e, src):
         to = (g + e) % G
-        return rc(lb.at[to], br.at[src], s_b.at[to], r_b.at[src], me, chip_of(st, to) * 2 + h)
+        return rc(lb.at[to], br.at[src], s_b, r_b, me, chip_of(st, to) * 2 + h)
 
     def send_b(e, c):
         b_copy(e, g).start()
@@ -328,26 +320,22 @@
     dec_rows.append(jnp.zeros((1, HALF), F32))
     decall[me] = jnp.concatenate(dec_rows, axis=0)
 
-    def wait_b(e, c):
-        b_copy(e, (g + e) % G).wait_recv()
-        return c
-
-    lax.fori_loop(1, G, wait_b, 0)
+    blocks(br, G - 1, s_b, r_b).wait_recv()
     gbuf[me, h, st] = br[...].reshape(R // 2, HALF).astype(BF16)
 
     def g_copy(off, k):
         ref = gbuf.at[k, h, st]
-        return rc(ref, ref, s_g.at[off], r_g.at[k], depth_peer(off), lat)
+        return rc(ref, ref, s_g, r_g.at[k], depth_peer(off), lat)
 
     def n_copy(d, s):
         ref = gbuf.at[d, h, s]
-        return rc(ref, ref, s_n.at[d], r_n.at[d], me, near)
+        return rc(ref, ref, s_n, r_n.at[d], me, near)
 
     def pb_copy(d, half):
-        return rc(gbuf.at[d, half], gbuf.at[d, half], s_pb.at[d], r_pb.at[d], me, sib)
+        return rc(gbuf.at[d, half], gbuf.at[d, half], s_pb, r_pb.at[d], me, sib)
 
     def d_copy(off, k):
-        return rc(decall.at[k], decall.at[k], s_d.at[off], r_d.at[k], depth_peer(off), lat)
+        return rc(decall.at[k], decall.at[k], s_d, r_d, depth_peer(off), lat)
 
     def send_g(i, c):
         g_copy(near_offset_of(i) % K, me).start()
@@ -426,7 +414,7 @@
     lax.fori_loop(0, K + PAIR_LAG, back_step, 0)
 
     def t_copy(off, k):
-        return rc(tmall.at[k], tmall.at[k], s_t.at[off], r_t.at[k], depth_peer(off), lat)
+        return rc(tmall.at[k], tmall.at[k], s_t, r_t, depth_peer(off), lat)
 
     def send_t(off, c):
         t_copy(off, me).start()
@@ -434,11 +422,7 @@
 
     lax.fori_loop(1, K, send_t, 0)
 
-    def wait_d(off, c):
-        d_copy(off, depth_peer(off)).wait_recv()
-        return c
-
-    lax.fori_loop(1, K, wait_d, 0)
+    blocks(decall, K - 1, s_d, r_d).wait_recv()
     dec_sum = decall[0]
     for k in range(1, K):
         dec_sum = dec_sum + decall[k]
@@ -450,7 +434,7 @@
 
     def e_copy(e, src):
         to = (m + e) % CHIPS
-        return rc(esend, elat.at[src], s_e.at[to], r_e.at[src], me, to * 2 + h)
+        return rc(esend, elat.at[src], s_e, r_e, me, to * 2 + h)
 
     def send_e(e, c):
         e_copy(e, m).start()
@@ -464,11 +448,7 @@
 
     lax.fori_loop(1, K, third_step, 0)
 
-    def wait_t(off, c):
-        t_copy(off, depth_peer(off)).wait_recv()
-        return c
-
-    lax.fori_loop(1, K, wait_t, 0)
+    blocks(tmall, K - 1, s_t, r_t).wait_recv()
     behind = jnp.zeros((K, R), F32)
     for k in range(K):
         behind = behind + tmall[k] * jnp.where(places[k] > mine, 1.0, 0.0)
@@ -484,11 +464,7 @@
         sig = 1.0 / (1.0 + jnp.exp(-lg))
         lgrad[d] = (density_grad * sig).astype(BF16).astype(F32)
 
-    def wait_e(e, c):
-        e_copy(e, (m + e) % CHIPS).wait_recv()
-        return c
-
-    lax.fori_loop(1, CHIPS, wait_e, 0)
+    blocks(elat, CHIPS - 1, s_e, r_e).wait_recv()
     err_sum = elat[0]
     for k in range(1, CHIPS):
         err_sum = err_sum + elat[k]
@@ -531,33 +507,18 @@
     ep_copy.wait_recv()
     err_ref[...] = (epsend[0:1, 0:1] + eprec[0:1, 0:1]) * (1.0 / COUNT)
 
-    def end_depth(off, c):
-        d = depth_peer(off)
-        ds_copy(off, me).wait_send()
-        z_copy(d, me).wait_send()
-        g_copy(off, me).wait_send()
-        d_copy(off, me).wait_send()
-        t_copy(off, me).wait_send()
-        l_copy(off, g).wait_send()
-        b_copy(off, g).wait_send()
-        return c
-
-    lax.fori_loop(1, K, end_depth, 0)
-
-    def end_lateral(e, c):
-        e_copy(e, m).wait_send()
-        return c
-
-    lax.fori_loop(1, CHIPS, end_lateral, 0)
-
-    def end_pair(d, c):
-        pf_copy(d).wait_send()
-        y_copy(d).wait_send()
-        n_copy(d, st).wait_send()
-        pb_copy(d, h).wait_send()
-        return c
-
-    lax.fori_loop(0, K, end_pair, 0)
+    blocks(dsall, K - 1, s_ds, r_ds).wait_send()
+    blocks(prec, K, s_pf, r_pf.at[0]).wait_send()
+    blocks(ysend, K, s_y, r_y.at[0]).wait_send()
+    blocks(zsend, K - 1, s_z, r_z).wait_send()
+    blocks(lt, G - 1, s_l, r_l).wait_send()
+    blocks(lb, G - 1, s_b, r_b).wait_send()
+    blocks(zsend, K - 1, s_g, r_g.at[0]).wait_send()
+    blocks(ysend, K, s_n, r_n.at[0]).wait_send()
+    blocks(prec, K, s_pb, r_pb.at[0]).wait_send()
+    blocks(decall, K - 1, s_d, r_d).wait_send()
+    blocks(tmall, K - 1, s_t, r_t).wait_send()
+    blocks(elat, CHIPS - 1, s_e, r_e).wait_send()
     ep_copy.wait_send()
 
 
@@ -617,18 +578,18 @@
             v((8, R), F32),
             v((8, R), F32),
             dma((S,)),
-            dma((K,)), dma((K,)),
-            dma((K,)), dma((K,)),
-            dma((K,)), dma((K,)),
-            dma((K,)), dma((K,)),
-            dma((G,)), dma((G,)),
-            dma((G,)), dma((G,)),
-            dma((K,)), dma((K,)),
-            dma((K,)), dma((K,)),
-            dma((K,)), dma((K,)),
-            dma((K,)), dma((K,)),
-            dma((K,)), dma((K,)),
-            dma((CHIPS,)), dma((CHIPS,)),
+            dma(()), dma(()),
+            dma(()), dma((K,)),
+            dma(()), dma((K,)),
+            dma(()), dma(()),
+            dma(()), dma(()),
+            dma(()), dma(()),
+            dma(()), dma((K,)),
+            dma(()), dma((K,)),
+            dma(()), dma((K,)),
+            dma(()), dma(()),
+            dma(()), dma(()),
+            dma(()), dma(()),
             dma(()), dma(()),
         ],
         compiler_params=pltpu.CompilerParams(

time: 70.4 us -> 68.3 us (0.970)
  Pallas kernels: 69.6 us -> 67.6 us
    pallas_call x1, Pallas kernels: 68 us -> 66 us  [body(): pl.pallas_call(kernel, name='step', out_shape=tuple((pltpu.VMEM(shape, F3...]
where the time goes in v5:
time: 68.3 us; the launch traced here: 68.2 us
  Pallas kernels  67.6 us (99%)
    pallas_call x1, Pallas kernels, body(): pl.pallas_call(kernel, name='step', out_shape=tuple((pltpu.VMEM(shape, F3...  66 us
    pallas_call x1, Pallas kernels, body(): pl.pallas_call(put_out, name='put_out', out_shape=tuple((jax.ShapeDtypeSt...  1.59 us

profile of v5, /device:TPU:1, one launch (start us, length us, event | category | flops | bytes accessed | tf_op | source)
XLA Modules:
  0.0 68.2 jit_solution(17267136712581019623)
XLA Ops:
  0.6 66.0 %step.1 = (f32[64,256]{1,0:T(8,128)S(1)}, f32[256,256]{1,0:T(8,128)S(1)}, f32[256,512]{1,0:T(8,128)S(1)}, f32[1,256]{1,0:T(1,128)S(1)}, f32[3,1,512]{2,1,0:T(1,128)S(1)}, /*index=5*/f32[1,1]{1,0:T(1,128)}) custom-call(bf16[64,8192]{1,0:T(8,128)(2,1)} %bitcast.13, bf16[64,256]{1,0:T(8,128)(2,1)} %bitcast.16, bf16[256,256]{1,0:T(8,128)(2,1)} %bitcast.15, ...), custom_call_target="tpu_custom_call" | custom-call | tf_op jit(solution)/shard_map/step/pallas_call | solution.py:535
  66.6 1.6 %put_out.1 = (f32[64,256]{1,0:T(8,128)}, f32[256,256]{1,0:T(8,128)}, f32[256,512]{1,0:T(8,128)}, f32[1,256]{1,0:T(1,128)}, f32[3,1,512]{2,1,0:T(1,128)}, /*index=5*/f32[1,1]{1,0:T(1,128)}) custom-call(f32[64,256]{1,0:T(8,128)S(1)} %get-tuple-element.18.refs_0_, f32[256,256]{1,0:T(8,128)S(1)} %get-tuple-element.19.refs_1_, ...), custom_call_target="tpu_custom_call" | custom-call | tf_op jit(solution)/shard_map/put_out/pallas_call | solution.py:609

commit v6 on v5

--- a/solution.py
+++ b/solution.py
@@ -42,12 +42,12 @@
 
 
 def kernel(
-    x_ref, w1_ref, w2_ref, w3_ref, wd_ref, dec_ref, order_ref, slot_ref, tgt_ref,
+    x_ref, w1_ref, w2_ref, w3_hbm, wd_ref, dec_ref, order_ref, slot_ref, tgt_ref,
     g1_ref, g2_ref, g3_ref, gd_ref, gdec_ref, err_ref,
-    xs, w1t, w2t, w3t, wdb, h1s, h2s, feats, lgs, wts, expi, bld, scl, scaled, oh,
+    w3_ref, xs, w1t, w2t, w3t, wdb, h1s, h2s, feats, lgs, wts, expi, bld, scl, scaled, oh,
     pfull, prec, ysend, yrec, zsend, zrecv, lt, lr, lb, br, gbuf, dsall, tmall, wgs, lgrad, b2s, b2t, b2p,
     decall, esend, elat, epsend, eprec,
-    s_x, s_ds, r_ds, s_pf, r_pf, s_y, r_y, s_z, r_z, s_l, r_l, s_b, r_b, s_g, r_g, s_n, r_n, s_pb, r_pb,
+    s_w, s_x, s_ds, r_ds, s_pf, r_pf, s_y, r_y, s_z, r_z, s_l, r_l, s_b, r_b, s_g, r_g, s_n, r_n, s_pb, r_pb,
     s_t, r_t, s_d, r_d, s_e, r_e, s_ep, r_ep,
 ):
     me = lax.axis_index("depth")
@@ -77,6 +77,8 @@
 
     for s in range(S):
         x_copy(s).start()
+    w3_copy = pltpu.make_async_copy(w3_hbm, w3_ref, s_w)
+    w3_copy.start()
 
     def blocks(ref, n, ssem, rsem):
         part = ref.at[pl.ds(0, n)]
@@ -101,7 +103,6 @@
     w1t[...] = w1_ref[...].T
     w2t[...] = w2_ref[...].T
     wd8 = jnp.broadcast_to(wd_ref[...], (8, HID))
-    wdb[...] = jnp.broadcast_to(wd_ref[...].astype(F32), (R, HID)).T
 
     def take_x(d):
         return jnp.concatenate(
@@ -129,21 +130,23 @@
     inc = density
     for sh in (1, 2, 4):
         inc = inc + jnp.where(sub >= sh, pltpu.roll(inc, sh, 1), 0.0)
+    dsall[me] = STEP * jnp.concatenate([inc[d, S - 1 : S, :] for d in range(K)], axis=0)
+
+    pl.semaphore_wait(barrier, K - 1 + CHIPS - 1 + 1)
+
+    def ds_copy(off, k):
+        return rc(dsall.at[k], dsall.at[k], s_ds, r_ds, depth_peer(off), lat)
+
+    def send_ds(off, c):
+        ds_copy(off, me).start()
+        return c
+
+    lax.fori_loop(1, K, send_ds, 0)
+    w3_copy.wait()
+    w3t[...] = w3_ref[...].T
+    wdb[...] = jnp.broadcast_to(wd_ref[...].astype(F32), (R, HID)).T
     wts[...] = jnp.exp(-STEP * (inc - density)) * (1.0 - jnp.exp(-STEP * density))
     expi[...] = jnp.exp(-STEP * inc)
-    dsall[me] = STEP * jnp.concatenate([inc[d, S - 1 : S, :] for d in range(K)], axis=0)
-
-    pl.semaphore_wait(barrier, K - 1 + CHIPS - 1 + 1)
-
-    def ds_copy(off, k):
-        return rc(dsall.at[k], dsall.at[k], s_ds, r_ds, depth_peer(off), lat)
-
-    def send_ds(off, c):
-        ds_copy(off, me).start()
-        return c
-
-    lax.fori_loop(1, K, send_ds, 0)
-    w3t[...] = w3_ref[...].T
 
     row = lax.broadcasted_iota(jnp.int32, (2 * R, R), 0)
     code = (chip_of((row // 64) % 2, (row // 8) % G) * 2 + row // R) * 4 + row % 4
@@ -529,6 +532,7 @@
 
 def body(samples, w_first, w_second, w_third, w_density, decoder, depth_order, ray_slot, target):
     vmem = pl.BlockSpec(memory_space=pltpu.VMEM)
+    hbm = pl.BlockSpec(memory_space=pl.ANY)
     dma = pltpu.SemaphoreType.DMA
     v = pltpu.VMEM
     results = ((ENC, HID), (HID, HID), (HID, FEAT), (1, HID), (3, 1, FEAT), (1, 1))
@@ -536,9 +540,10 @@
         kernel,
         name="step",
         out_shape=tuple(pltpu.VMEM(shape, F32) for shape in results),
-        in_specs=[pl.BlockSpec(memory_space=pl.ANY)] + [vmem] * 5 + [pl.BlockSpec(memory_space=pltpu.SMEM)] + [vmem] * 2,
+        in_specs=[hbm, vmem, vmem, hbm, vmem, vmem] + [pl.BlockSpec(memory_space=pltpu.SMEM)] + [vmem] * 2,
         out_specs=(vmem,) * 6,
         scratch_shapes=[
+            v((HID, FEAT), BF16),
             v((S, ENC, K * R), BF16),
             v((HID, ENC), BF16),
             v((HID, HID), BF16),
@@ -577,6 +582,7 @@
             v((CHIPS, 8, R), F32),
             v((8, R), F32),
             v((8, R), F32),
+            dma(()),
             dma((S,)),
             dma(()), dma(()),
             dma(()), dma((K,)),

time: 68.3 us -> 68.2 us (level)
  no operation moved by 1% of the time
where the time goes in v6:
time: 68.2 us; the launch traced here: 68 us
  Pallas kernels  67.4 us (99%)
    pallas_call x1, Pallas kernels, body(): pl.pallas_call(kernel, name='step', out_shape=tuple((pltpu.VMEM(shape, F3...  65.8 us
    pallas_call x1, Pallas kernels, body(): pl.pallas_call(put_out, name='put_out', out_shape=tuple((jax.ShapeDtypeSt...  1.59 us

profile of v6, /device:TPU:1, one launch (start us, length us, event | category | flops | bytes accessed | tf_op | source)
XLA Modules:
  0.0 68.0 jit_solution(10145449901887697271)
XLA Ops:
  0.6 65.8 %step.1 = (f32[64,256]{1,0:T(8,128)S(1)}, f32[256,256]{1,0:T(8,128)S(1)}, f32[256,512]{1,0:T(8,128)S(1)}, f32[1,256]{1,0:T(1,128)S(1)}, f32[3,1,512]{2,1,0:T(1,128)S(1)}, /*index=5*/f32[1,1]{1,0:T(1,128)}) custom-call(bf16[64,8192]{1,0:T(8,128)(2,1)} %bitcast.13, bf16[64,256]{1,0:T(8,128)(2,1)} %bitcast.16, bf16[256,256]{1,0:T(8,128)(2,1)} %bitcast.15, ...), custom_call_target="tpu_custom_call" | custom-call | tf_op jit(solution)/shard_map/step/pallas_call | solution.py:539
  66.5 1.6 %put_out.1 = (f32[64,256]{1,0:T(8,128)}, f32[256,256]{1,0:T(8,128)}, f32[256,512]{1,0:T(8,128)}, f32[1,256]{1,0:T(1,128)}, f32[3,1,512]{2,1,0:T(1,128)}, /*index=5*/f32[1,1]{1,0:T(1,128)}) custom-call(f32[64,256]{1,0:T(8,128)S(1)} %get-tuple-element.18.refs_0_, f32[256,256]{1,0:T(8,128)S(1)} %get-tuple-element.19.refs_1_, ...), custom_call_target="tpu_custom_call" | custom-call | tf_op jit(solution)/shard_map/put_out/pallas_call | solution.py:615
